TPU v7x, 32 devices: a whole 2x2x4 slice. The times are simulated.
32 devices in a mesh: grp: 2 (over x), res: 16 (over z, y, core).
Axes of the slice: x: 2, y: 2, z: 4, core: 2. Of those that a mesh axis runs over, the one named last changes fastest.
Arguments:
- alignment_activations: bfloat16 [128, 128, 256], P('grp', 'res'), parts along dimension 0, may hold values from -6 to 6
- projection_weight: bfloat16 [256, 64], replicated, may hold values from -0.375 to 0.375
- output_weight: bfloat16 [1024, 128], replicated, may hold values from -0.1875 to 0.1875
- output_bias: float32 [128], replicated, may hold values from -3 to 3
- pair_update_gradient: bfloat16 [256, 128, 128], P(('grp', 'res')), parts along dimension 0, may hold values from -6 to 6
- sequence_mask: int32 [128], P('grp'), parts along dimension 0, may hold values 0 or 1
- residue_mask: int32 [256], P('grp'), parts along dimension 0, may hold values 0 or 1
Outputs:
- pair_increment: bfloat16 [256, 128, 128], P(('grp', 'res')), parts along dimension 0
- alignment_gradient: bfloat16 [128, 128, 256], P('grp', 'res'), parts along dimension 0
There are 2 independent parts, one for each index of `grp`. A program takes and returns all parts, laid end to end along the dimension named above; an argument that names none is the same for every part. Nothing has to cross between parts.
All inputs are finite; a program needn't handle non-finite values.
Results may differ from a plain program's by a relative error of at most 0.007.
Values may be sent and summed in bfloat16 or wider, within the bound.
No kernel may reach another device: no remote copies, remote signals or barrier semaphores. Data moves between devices by JAX's collectives and lax.ppermute only.
A program may use at most 64 MiB of HBM per device.

v0:
```python
import jax
import jax.numpy as jnp
from jax import lax
from jax.sharding import PartitionSpec as P

eps_norm = 1e-05


def layer_norm_forward(values):
    mean_val = jnp.mean(values, axis=-1, keepdims=True)
    centered = values - mean_val
    inverse_deviation = lax.rsqrt(jnp.mean(centered * centered, axis=-1, keepdims=True) + eps_norm)
    return (centered * inverse_deviation, inverse_deviation)


def layer_norm_backward(grad_out, scaled_product, inverse_deviation):
    mean_grad = jnp.mean(grad_out, axis=-1, keepdims=True)
    mean_cross = jnp.mean(grad_out * scaled_product, axis=-1, keepdims=True)
    return inverse_deviation * (grad_out - mean_grad - scaled_product * mean_cross)


def body(
    alignment_activations,
    projection_weight,
    output_weight,
    output_bias,
    pair_update_gradient,
    sequence_mask,
    residue_mask,
):
    alignment_rows = alignment_activations.shape[0]
    local_rows = alignment_activations.shape[1]
    alignment_width = alignment_activations.shape[2]
    projected_width = projection_weight.shape[1] // 2
    pair_width = output_weight.shape[1]
    row_start = lax.axis_index("res") * local_rows
    residue_float_mask = residue_mask.astype(jnp.float32)
    local_residues = lax.dynamic_slice_in_dim(residue_float_mask, row_start, local_rows)
    alignment_mask = sequence_mask.astype(jnp.float32)[:, None] * local_residues[None, :]
    scaled_product, inverse_deviation = layer_norm_forward(
        alignment_activations.astype(jnp.float32)
    )
    normalized_input = scaled_product.astype(jnp.bfloat16)
    projected_rows = jnp.dot(
        normalized_input.reshape(-1, alignment_width),
        projection_weight,
        preferred_element_type=jnp.float32,
    )
    projected_rows = (
        projected_rows.reshape(alignment_rows, local_rows, 2 * projected_width)
        * alignment_mask[:, :, None]
    )
    projected_rows = projected_rows.astype(jnp.bfloat16)
    left_projected = projected_rows[:, :, :projected_width]
    right_proj = projected_rows[:, :, projected_width:]
    live_rows = jnp.sum(sequence_mask.astype(jnp.float32))
    right_all = lax.all_gather(right_proj, "res", axis=1, tiled=True)
    residue_count = right_all.shape[1]
    block_columns = 256 if residue_count % 256 == 0 else residue_count
    block_count = residue_count // block_columns
    count_rows = jnp.maximum(live_rows * local_residues[:, None] * residue_float_mask[None, :], 1.0)

    def pair_block(carry, block_id):
        pair_increment, left_gradient, gradient_pieces = carry
        column_offset = block_id * block_columns
        right_blk = lax.dynamic_slice_in_dim(right_all, column_offset, block_columns, 1)
        cot_blk = lax.dynamic_slice_in_dim(pair_update_gradient, column_offset, block_columns, 1)
        count_blk = lax.dynamic_slice_in_dim(count_rows, column_offset, block_columns, 1)
        outer = jnp.einsum(
            "sic,sjd->ijcd", left_projected, right_blk, preferred_element_type=jnp.float32
        )
        outer = outer.astype(jnp.bfloat16).reshape(-1, projected_width * projected_width)
        update = jnp.dot(outer, output_weight, preferred_element_type=jnp.float32)
        update = update.reshape(local_rows, block_columns, pair_width) + output_bias
        update = (update / count_blk[:, :, None]).astype(jnp.bfloat16)
        pair_increment = lax.dynamic_update_slice_in_dim(pair_increment, update, column_offset, 1)
        grad_outer = jnp.dot(
            cot_blk.reshape(-1, pair_width), output_weight.T, preferred_element_type=jnp.float32
        )
        grad_outer = (
            grad_outer.reshape(local_rows, block_columns, projected_width, projected_width)
            / count_blk[:, :, None, None]
        )
        grad_outer = grad_outer.astype(jnp.bfloat16)
        left_gradient = left_gradient + jnp.einsum(
            "ijcd,sjd->sic", grad_outer, right_blk, preferred_element_type=jnp.float32
        )
        gradient_piece = jnp.einsum(
            "ijcd,sic->jsd", grad_outer, left_projected, preferred_element_type=jnp.float32
        )
        gradient_pieces = lax.dynamic_update_slice_in_dim(
            gradient_pieces,
            gradient_piece.reshape(block_columns, alignment_rows * projected_width),
            column_offset,
            0,
        )
        return ((pair_increment, left_gradient, gradient_pieces), None)

    start_update = jnp.zeros((local_rows, residue_count, pair_width), jnp.bfloat16)
    initial_left = jnp.zeros((alignment_rows, local_rows, projected_width), jnp.float32)
    initial_pieces = jnp.zeros((residue_count, alignment_rows * projected_width), jnp.float32)
    (pair_increment, left_gradient, gradient_pieces), unused = lax.scan(
        pair_block, (start_update, initial_left, initial_pieces), jnp.arange(block_count)
    )
    gradient_total = lax.psum_scatter(gradient_pieces, "res", scatter_dimension=0, tiled=True)
    right_gradient = gradient_total.reshape(local_rows, alignment_rows, projected_width).transpose(
        1, 0, 2
    )
    projection_gradient = (
        jnp.concatenate([left_gradient, right_gradient], axis=-1) * alignment_mask[:, :, None]
    )
    projection_gradient = projection_gradient.astype(jnp.bfloat16)
    normalized_gradient = jnp.dot(
        projection_gradient.reshape(-1, 2 * projected_width),
        projection_weight.T,
        preferred_element_type=jnp.float32,
    )
    normalized_gradient = normalized_gradient.reshape(alignment_rows, local_rows, alignment_width)
    alignment_gradient = layer_norm_backward(
        normalized_gradient, scaled_product, inverse_deviation
    ).astype(jnp.bfloat16)
    return (pair_increment, alignment_gradient)


def solution(mesh):
    in_specs = (
        P("grp", "res", None),
        P(),
        P(),
        P(),
        P(("grp", "res"), None, None),
        P("grp"),
        P("grp"),
    )
    out_specs = (P(("grp", "res"), None, None), P("grp", "res", None))
    return jax.shard_map(body, mesh=mesh, in_specs=in_specs, out_specs=out_specs, check_vma=False)
```

profile of v0, /device:TPU:0, one launch (start us, length us, event | category | flops | bytes accessed | tf_op | source)
XLA Modules:
  0.0 89.6 jit_solution(17013610262894951195)
XLA Ops:
  7.2 0.0 copy-start
  7.2 0.0 copy-start.7
  7.2 0.0 reduce-scatter.4.cloned.1.call-start
  7.2 1.3 %convert_reduce_fusion.1 = f32[]{:T(128)} fusion(s32[64]{0:T(128)} %param.12), kind=kLoop, calls=%fused_computation.46 | loop fusion | flops 127 | bytes 260 | tf_op jit(solution)/shard_map/reduce_sum | solution.py:56
  8.5 0.7 convert_element_type.41
  9.2 0.7 convert_element_type.42
  9.9 1.1 %convert_reduce_fusion = f32[64,8]{1,0:T(8,128)S(1)} fusion(bf16[64,8,256]{2,1,0:T(8,128)(2,1)} %param.7), kind=kLoop, calls=%fused_computation.15 | loop fusion | flops 261632 | bytes 264192 | tf_op jit(solution)/shard_map/reduce_sum | solution.py:10
  11.0 1.2 %fusion.23 = f32[64,8]{1,0:T(8,128)S(1)} fusion(bf16[64,8,256]{2,1,0:T(8,128)(2,1)} %param.7, f32[64,8]{1,0:T(8,128)S(1)} %broadcast_multiply_fusion.3), kind=kLoop, calls=%fused_computation.25 | loop fusion | flops 523776 | bytes 266240 | tf_op jit(solution)/shard_map/reduce_sum | solution.py:12
  12.2 0.7 broadcast_multiply_fusion.4
  12.9 0.1 add_rsqrt_fusion
  13.0 0.0 copy-start.4
  13.0 0.6 copy-done.4
  13.6 1.3 %fusion.9 = bf16[64,8,64]{2,1,0:T(8,128)(2,1)S(1)} fusion(bf16[64,8,256]{2,1,0:T(8,128)(2,1)} %param.7, f32[64,8]{1,0:T(8,128)S(1)} %get-tuple-element.29, f32[64,8]{1,0:T(8,128)S(1)} %broadcast_multiply_fusion.3, f32[64,8]{1,0:T(8,128)S(1)} %get-tuple-element.40, bf16[256,64]{0,1:T(8,128)(2,1)} %param.8), kind=kOutput, calls=%fused_computation.11 | convolution fusion | flops 17367040 | bytes 366592 | tf_op jit(solution)/shard_map/dot_general | solution.py:44
  14.8 0.1 fusion.39
  14.9 0.1 copy.23
  15.1 0.1 multiply_maximum_fusion
  15.2 0.0 copy-done
  15.2 0.0 copy-done.7
  15.2 0.7 divide_convert_fusion
  15.9 0.0 copy-start.2
  15.9 0.8 fusion.4
  16.7 0.6 copy.30
  17.3 0.0 copy-done.2
  17.3 1.3 %copy.43 = f32[128,2048]{1,0:T(8,128)} copy(f32[128,2048]{0,1:T(8,128)S(1)} %bitcast.49) | data formatting | bytes 2097152
  18.6 0.0 reduce-scatter.4.cloned.1.call-update
  18.7 32.3 %all_gather.3 = bf16[64,128,32]{2,1,0:T(8,128)(2,1)S(1)} all-gather(bf16[64,8,32]{2,1,0:T(8,128)(2,1)S(1)} %get-tuple-element.27), channel_id=1, replica_groups=mesh['grp'=2,'res'=16] {'res'}, dimensions={1}, use_global_device_ids=true | all-gather | bytes 557056 | tf_op jit(solution)/shard_map/all_gather | solution.py:57
  51.0 3.2 %copy.26 = bf16[64,128,32]{0,1,2:T(8,128)(2,1)S(1)} copy(bf16[64,128,32]{2,1,0:T(8,128)(2,1)S(1)} %all_gather.3) | data formatting | bytes 1048576 | tf_op jit(solution)/shard_map/all_gather | solution.py:57
  54.1 3.0 %fusion.10 = f32[64,8,32]{0,2,1:T(8,128)} fusion(bf16[8,128,32,32]{1,3,2,0:T(8,128)(2,1)} %copy-done.2, bf16[64,128,32]{0,1,2:T(8,128)(2,1)S(1)} %copy.26), kind=kOutput, calls=%fused_computation.12 | convolution fusion | flops 134217728 | bytes 2686976 | tf_op jit(solution)/shard_map/while/body/eval_jaxpr/ijcd,sjd->sic/dot_general | solution.py:85
  57.1 1.7 %copy.33 = f32[64,8,32]{2,1,0:T(8,128)} copy(f32[64,8,32]{0,2,1:T(8,128)} %fusion.10) | data formatting | bytes 131072 | tf_op jit(solution)/shard_map/while/body/eval_jaxpr/ijcd,sjd->sic/dot_general | solution.py:85
  58.9 3.2 %copy.34 = bf16[64,128,32,1]{0,1,3,2:T(8,128)(2,1)S(1)} copy(bf16[64,128,32,1]{2,1,0,3:T(8,128)(2,1)S(1)} %bitcast.47) | data formatting | bytes 1048576 | tf_op jit(solution)/shard_map/all_gather | solution.py:57
  62.1 0.7 convert_bitcast_fusion
  62.8 0.0 copy-start.8
  62.8 1.4 %copy.24 = bf16[8,128,32,32]{1,3,2,0:T(8,128)(2,1)S(1)} copy(bf16[8,128,32,32]{1,2,0,3:T(8,128)(2,1)S(1)} %convert_bitcast_fusion) | data formatting | bytes 4194304 | tf_op jit(solution)/shard_map/while/body/eval_jaxpr/convert_element_type | solution.py:72
  64.1 0.0 copy-done.8
  64.2 1.5 %fusion.8 = bf16[8,128,128]{2,1,0:T(8,128)(2,1)} fusion(bf16[8,128,1024]{1,2,0:T(8,128)(2,1)S(1)} %bitcast.50, bf16[1024,128]{1,0:T(8,128)(2,1)S(1)} %copy-done, f32[8,128]{1,0:T(8,128)S(1)} %multiply_maximum_fusion, f32[128]{0:T(128)S(1)} %copy-done.8), kind=kOutput, calls=%fused_computation.9 | convolution fusion | flops 268828672 | bytes 2626048 | tf_op jit(solution)/shard_map/while/body/eval_jaxpr/dot_general | solution.py:73
  65.6 0.0 copy-start.1
  65.7 0.0 copy-start.3
  65.7 0.0 copy-start.5
  65.7 0.0 copy-start.6
  65.7 14.0 %reduce-scatter.4.cloned.1.call-done = f32[8,2048]{1,0:T(8,128)} async-done(((f32[128,2048]{1,0:T(8,128)}), f32[8,2048]{1,0:T(8,128)}) %reduce-scatter.4.cloned.1.call-update) | async-done | bytes 65552
  79.7 1.2 %copy.44 = f32[8,2048]{0,1:T(8,128)S(1)} copy(f32[8,2048]{1,0:T(8,128)} %reduce-scatter.4.cloned.1.call-done) | data formatting | bytes 131072
  80.9 0.3 copy.32
  81.2 0.0 copy-done.1
  81.2 0.0 copy-done.3
  81.2 0.0 copy-done.5
  81.2 0.0 copy-done.6
  81.2 0.5 fusion.38
  81.8 1.0 %fusion.22 = bf16[64,8,256]{2,1,0:T(8,128)(2,1)} fusion(bf16[64,8,256]{2,1,0:T(8,128)(2,1)S(1)} %copy-done.1, f32[64,8,256]{2,1,0:T(8,128)S(1)} %get-tuple-element.28, f32[64,8]{1,0:T(8,128)S(1)} %broadcast_multiply_fusion.1, f32[64,8]{1,0:T(8,128)S(1)} %broadcast_multiply_fusion.2, f32[64,8]{1,0:T(8,128)S(1)} %get-tuple-element.29, ...), kind=kLoop, calls=%fused_computation.24 | loop fusion | flops 1048576 | bytes 1056768 | tf_op jit(solution)/shard_map/convert_element_type | solution.py:121
  (3 shorter events, 0.0 us)
Async XLA Ops:
  7.2 8.0 %copy-start = (bf16[1024,128]{1,0:T(8,128)(2,1)S(1)}, bf16[1024,128]{1,0:T(8,128)(2,1)}, u32[]{:S(2)}) copy-start(bf16[1024,128]{1,0:T(8,128)(2,1)} %param.9) | copy-start | bytes 786436
  7.2 8.0 %copy-start.7 = (bf16[8,128,128]{2,1,0:T(8,128)(2,1)S(1)}, bf16[8,128,128]{2,1,0:T(8,128)(2,1)}, u32[]{:S(2)}) copy-start(bf16[8,128,128]{2,1,0:T(8,128)(2,1)} %param.11) | copy-start | bytes 786436
  7.2 72.5 %reduce-scatter.4.cloned.1.call-start = ((), (), s32[]{:S(2)}) async-start(), calls=%async_computation.1 | async-start | bytes 1114112
  13.0 0.6 copy-start.4
  15.9 1.4 %copy-start.2 = (bf16[8,128,32,32]{1,3,2,0:T(8,128)(2,1)}, bf16[8,128,32,32]{1,3,2,0:T(8,128)(2,1)S(1)}, u32[]{:S(2)}) copy-start(bf16[8,128,32,32]{1,3,2,0:T(8,128)(2,1)S(1)} %divide_convert_fusion) | copy-start | bytes 6291460
  62.8 1.4 %copy-start.8 = (f32[128]{0:T(128)S(1)}, f32[128]{0:T(128)}, u32[]{:S(2)}) copy-start(f32[128]{0:T(128)} %param.10) | copy-start | bytes 1540
  65.6 15.5 %copy-start.1 = (bf16[64,8,256]{2,1,0:T(8,128)(2,1)S(1)}, bf16[64,8,256]{2,1,0:T(8,128)(2,1)}, u32[]{:S(2)}) copy-start(bf16[64,8,256]{2,1,0:T(8,128)(2,1)} %param.7) | copy-start | bytes 786436
  65.7 15.5 %copy-start.3 = (f32[64,8,32]{2,1,0:T(8,128)S(1)}, f32[64,8,32]{2,1,0:T(8,128)}, u32[]{:S(2)}) copy-start(f32[64,8,32]{2,1,0:T(8,128)} %copy.33) | copy-start | bytes 196612
  65.7 15.5 %copy-start.5 = (f32[64,8]{1,0:T(8,128)S(1)}, f32[64,8]{1,0:T(8,128)}, u32[]{:S(2)}) copy-start(f32[64,8]{1,0:T(8,128)} %copy-done.4) | copy-start | bytes 6148
  65.7 15.6 %copy-start.6 = (bf16[256,64]{0,1:T(8,128)(2,1)S(1)}, bf16[256,64]{0,1:T(8,128)(2,1)}, u32[]{:S(2)}) copy-start(bf16[256,64]{0,1:T(8,128)(2,1)} %param.8) | copy-start | bytes 98308
Sparse Core Ops, SparseCore 0:
  18.8 60.8 reduce-scatter.3
where the time goes:
time: 90 us; the launch traced here: 89.6 us
  blocking collectives  32.3 us (36%)
  between operations  14.2 us (16%)
  waiting for transfers between devices  14 us (16%)
  local copies, waits for them, and re-layouts  13.8 us (15%)
  matrix products  8.48 us (9%)
  other arithmetic  6.82 us (8%)
    all_gather x1, blocking collectives, body(): right_all = lax.all_gather(right_proj, 'res', axis=1, tiled=True)  32.3 us
    unnamed x2, waiting for transfers between devices  14 us
    all_gather x2, local copies, waits for them, and re-layouts, body(): right_all = lax.all_gather(right_proj, 'res', axis=1, tiled=True)  6.35 us
    unnamed x20, local copies, waits for them, and re-layouts  3.13 us
    dot_general x1, matrix products, pair_block(): jnp.einsum('ijcd,sjd->sic', grad_outer, right_blk, preferred_element_type...  2.99 us
  transfers between devices with their start and end apart: 1, of which 1 were waited for; matrix products, arithmetic and copies ran while one was open for 16% of the time, Pallas kernels for 0%

commit v1 on v0

--- a/solution.py
+++ b/solution.py
@@ -4,6 +4,16 @@
 from jax.sharding import PartitionSpec as P
 
 eps_norm = 1e-05
+
+
+def ring_gather(x, axis, dim):
+    ways, here, step = (lax.axis_size(axis), lax.axis_index(axis), x.shape[dim])
+    lengths = [n * ways if d == dim else n for d, n in enumerate(x.shape)]
+    full = lax.dynamic_update_slice_in_dim(jnp.zeros(lengths, x.dtype), x, here * step, axis=dim)
+    for far in range(1, ways):
+        x = lax.ppermute(x, axis, [(d, (d + 1) % ways) for d in range(ways)])
+        full = lax.dynamic_update_slice_in_dim(full, x, (here - far) % ways * step, axis=dim)
+    return full
 
 
 def layer_norm_forward(values):
@@ -54,7 +64,7 @@
     left_projected = projected_rows[:, :, :projected_width]
     right_proj = projected_rows[:, :, projected_width:]
     live_rows = jnp.sum(sequence_mask.astype(jnp.float32))
-    right_all = lax.all_gather(right_proj, "res", axis=1, tiled=True)
+    right_all = ring_gather(right_proj, "res", 1)
     residue_count = right_all.shape[1]
     block_columns = 256 if residue_count % 256 == 0 else residue_count
     block_count = residue_count // block_columns

time: 90 us -> 282 us (3.13)
  local copies, waits for them, and re-layouts: 13.8 us -> 151 us
  waiting for transfers between devices: 14 us -> 102 us
  blocking collectives: 32.3 us -> 0 us
    dynamic_update_slice x0 -> x16, local copies, waits for them, and re-layouts: none -> 115 us  [the longest x15 112 us: ring_gather(): lax.dynamic_update_slice_in_dim(full, x, (here - far) % ways * step, axis...]
    ppermute x0 -> x15, waiting for transfers between devices: none -> 102 us  [ring_gather(): x = lax.ppermute(x, axis, [(d, (d + 1) % ways) for d in range(ways)])]
    all_gather x1 -> x0, blocking collectives: 32.3 us -> none  [body(): right_all = lax.all_gather(right_proj, 'res', axis=1, tiled=True)]
    ppermute x0 -> x15, local copies, waits for them, and re-layouts: none -> 26.8 us  [ring_gather(): x = lax.ppermute(x, axis, [(d, (d + 1) % ways) for d in range(ways)])]
    unnamed x2, waiting for transfers between devices: 14 us -> 0.02 us
    all_gather x2 -> x0, local copies, waits for them, and re-layouts: 6.35 us -> none  [body(): right_all = lax.all_gather(right_proj, 'res', axis=1, tiled=True)]
  transfers between devices with their start and end apart: 1 -> 16, of which waited for: 1 -> 14; matrix products, arithmetic and copies ran while one was open for 16% -> 53% of each run, Pallas kernels for 0% -> 0%
where the time goes in v1:
time: 282 us
  local copies, waits for them, and re-layouts  151 us (54%)
  waiting for transfers between devices  102 us (36%)
  between operations  14.9 us (5%)
  other arithmetic  6.82 us (2%)
  matrix products  6.16 us (2%)
    dynamic_update_slice x15, local copies, waits for them, and re-layouts, ring_gather(): lax.dynamic_update_slice_in_dim(full, x, (here - far) % ways * step, axis...  112 us
    ppermute x15, waiting for transfers between devices, ring_gather(): x = lax.ppermute(x, axis, [(d, (d + 1) % ways) for d in range(ways)])  102 us
    ppermute x15, local copies, waits for them, and re-layouts, ring_gather(): x = lax.ppermute(x, axis, [(d, (d + 1) % ways) for d in range(ways)])  26.8 us
  transfers between devices with their start and end apart: 16, of which 14 were waited for; matrix products, arithmetic and copies ran while one was open for 53% of the time, Pallas kernels for 0%

profile of v1, /device:TPU:0, one launch (start us, length us, event | category | flops | bytes accessed | tf_op | source)
XLA Modules:
  0.0 281.6 jit_solution(12178421674492515662)
XLA Ops:
  7.2 1.3 convert_reduce_fusion.1
  8.5 0.7 convert_element_type.41
  9.2 0.7 convert_element_type.42
  9.9 1.1 convert_reduce_fusion
  11.0 1.2 fusion.22
  12.2 0.7 broadcast_multiply_fusion.4
  13.6 1.3 fusion.9
  14.8 0.8 fusion.40
  15.8 0.7 divide_convert_fusion
  16.5 0.8 fusion.4
  18.0 1.3 copy.85
  19.9 8.0 %collective-permute-done = bf16[64,8,32]{2,1,0:T(8,128)(2,1)} collective-permute-done((bf16[64,8,32]{2,1,0:T(8,128)(2,1)}, bf16[64,8,32]{2,1,0:T(8,128)(2,1)}, u32[]{:S(2)}, u32[]{:S(2)}) %collective-permute-start) | collective-permute-done | bytes 32800 | tf_op jit(solution)/shard_map/ppermute | solution.py:14
  27.8 7.4 %collective-permute-done.1 = bf16[64,8,32]{2,1,0:T(8,128)(2,1)} collective-permute-done((bf16[64,8,32]{2,1,0:T(8,128)(2,1)}, bf16[64,8,32]{2,1,0:T(8,128)(2,1)}, u32[]{:S(2)}, u32[]{:S(2)}) %collective-permute-start.1) | collective-permute-done | bytes 32800 | tf_op jit(solution)/shard_map/ppermute | solution.py:14
  35.2 7.4 %collective-permute-done.2 = bf16[64,8,32]{2,1,0:T(8,128)(2,1)} collective-permute-done((bf16[64,8,32]{2,1,0:T(8,128)(2,1)}, bf16[64,8,32]{2,1,0:T(8,128)(2,1)}, u32[]{:S(2)}, u32[]{:S(2)}) %collective-permute-start.2) | collective-permute-done | bytes 32800 | tf_op jit(solution)/shard_map/ppermute | solution.py:14
  42.6 7.3 %collective-permute-done.3 = bf16[64,8,32]{2,1,0:T(8,128)(2,1)S(1)} collective-permute-done((bf16[64,8,32]{2,1,0:T(8,128)(2,1)}, bf16[64,8,32]{2,1,0:T(8,128)(2,1)S(1)}, u32[]{:S(2)}, u32[]{:S(2)}) %collective-permute-start.3) | collective-permute-done | bytes 32800 | tf_op jit(solution)/shard_map/ppermute | solution.py:14
  49.9 7.3 %collective-permute-done.4 = bf16[64,8,32]{2,1,0:T(8,128)(2,1)S(1)} collective-permute-done((bf16[64,8,32]{2,1,0:T(8,128)(2,1)S(1)}, bf16[64,8,32]{2,1,0:T(8,128)(2,1)S(1)}, u32[]{:S(2)}, u32[]{:S(2)}) %collective-permute-start.4) | collective-permute-done | bytes 32800 | tf_op jit(solution)/shard_map/ppermute | solution.py:14
  57.2 7.2 %collective-permute-done.5 = bf16[64,8,32]{2,1,0:T(8,128)(2,1)S(1)} collective-permute-done((bf16[64,8,32]{2,1,0:T(8,128)(2,1)S(1)}, bf16[64,8,32]{2,1,0:T(8,128)(2,1)S(1)}, u32[]{:S(2)}, u32[]{:S(2)}) %collective-permute-start.5) | collective-permute-done | bytes 32800 | tf_op jit(solution)/shard_map/ppermute | solution.py:14
  64.4 7.2 %collective-permute-done.6 = bf16[64,8,32]{2,1,0:T(8,128)(2,1)S(1)} collective-permute-done((bf16[64,8,32]{2,1,0:T(8,128)(2,1)S(1)}, bf16[64,8,32]{2,1,0:T(8,128)(2,1)S(1)}, u32[]{:S(2)}, u32[]{:S(2)}) %collective-permute-start.6) | collective-permute-done | bytes 32800 | tf_op jit(solution)/shard_map/ppermute | solution.py:14
  71.6 7.4 %collective-permute-done.7 = bf16[64,8,32]{2,1,0:T(8,128)(2,1)S(1)} collective-permute-done((bf16[64,8,32]{2,1,0:T(8,128)(2,1)S(1)}, bf16[64,8,32]{2,1,0:T(8,128)(2,1)S(1)}, u32[]{:S(2)}, u32[]{:S(2)}) %collective-permute-start.7) | collective-permute-done | bytes 32800 | tf_op jit(solution)/shard_map/ppermute | solution.py:14
  79.0 7.1 %collective-permute-done.8 = bf16[64,8,32]{2,1,0:T(8,128)(2,1)S(1)} collective-permute-done((bf16[64,8,32]{2,1,0:T(8,128)(2,1)S(1)}, bf16[64,8,32]{2,1,0:T(8,128)(2,1)S(1)}, u32[]{:S(2)}, u32[]{:S(2)}) %collective-permute-start.8) | collective-permute-done | bytes 32800 | tf_op jit(solution)/shard_map/ppermute | solution.py:14
  86.1 7.1 %collective-permute-done.9 = bf16[64,8,32]{2,1,0:T(8,128)(2,1)S(1)} collective-permute-done((bf16[64,8,32]{2,1,0:T(8,128)(2,1)S(1)}, bf16[64,8,32]{2,1,0:T(8,128)(2,1)S(1)}, u32[]{:S(2)}, u32[]{:S(2)}) %collective-permute-start.9) | collective-permute-done | bytes 32800 | tf_op jit(solution)/shard_map/ppermute | solution.py:14
  93.2 7.1 %collective-permute-done.10 = bf16[64,8,32]{2,1,0:T(8,128)(2,1)S(1)} collective-permute-done((bf16[64,8,32]{2,1,0:T(8,128)(2,1)S(1)}, bf16[64,8,32]{2,1,0:T(8,128)(2,1)S(1)}, u32[]{:S(2)}, u32[]{:S(2)}) %collective-permute-start.10) | collective-permute-done | bytes 32800 | tf_op jit(solution)/shard_map/ppermute | solution.py:14
  100.3 7.1 %collective-permute-done.11 = bf16[64,8,32]{2,1,0:T(8,128)(2,1)S(1)} collective-permute-done((bf16[64,8,32]{2,1,0:T(8,128)(2,1)S(1)}, bf16[64,8,32]{2,1,0:T(8,128)(2,1)S(1)}, u32[]{:S(2)}, u32[]{:S(2)}) %collective-permute-start.11) | collective-permute-done | bytes 32800 | tf_op jit(solution)/shard_map/ppermute | solution.py:14
  107.4 0.6 copy-done.10
  108.1 7.1 %collective-permute-done.12 = bf16[64,8,32]{2,1,0:T(8,128)(2,1)S(1)} collective-permute-done((bf16[64,8,32]{2,1,0:T(8,128)(2,1)S(1)}, bf16[64,8,32]{2,1,0:T(8,128)(2,1)S(1)}, u32[]{:S(2)}, u32[]{:S(2)}) %collective-permute-start.12) | collective-permute-done | bytes 32800 | tf_op jit(solution)/shard_map/ppermute | solution.py:14
  115.8 7.2 %collective-permute-done.13 = bf16[64,8,32]{2,1,0:T(8,128)(2,1)} collective-permute-done((bf16[64,8,32]{2,1,0:T(8,128)(2,1)S(1)}, bf16[64,8,32]{2,1,0:T(8,128)(2,1)}, u32[]{:S(2)}, u32[]{:S(2)}) %collective-permute-start.13) | collective-permute-done | bytes 32800 | tf_op jit(solution)/shard_map/ppermute | solution.py:14
  123.0 1.8 copy.52
  125.3 2.5 dynamic_update_slice.52
  127.9 1.8 copy.53
  129.6 7.5 %dynamic_update_slice.53 = bf16[64,128,32]{1,0,2:T(8,128)(2,1)S(1)} dynamic-update-slice(bf16[64,128,32]{1,0,2:T(8,128)(2,1)S(1)} %dynamic_update_slice.52, bf16[64,8,32]{1,0,2:T(8,128)(2,1)S(1)} %copy.53, s32[]{:T(128)} %constant.128.clone.1, s32[]{:T(128)S(6)} %select_n.120, s32[]{:T(128)} %constant.128.clone.1) | dynamic-update-slice | bytes 65540 | tf_op jit(solution)/shard_map/dynamic_update_slice | solution.py:15
  137.1 1.8 copy.54
  138.9 7.5 %dynamic_update_slice.54 = bf16[64,128,32]{1,0,2:T(8,128)(2,1)S(1)} dynamic-update-slice(bf16[64,128,32]{1,0,2:T(8,128)(2,1)S(1)} %dynamic_update_slice.53, bf16[64,8,32]{1,0,2:T(8,128)(2,1)S(1)} %copy.54, s32[]{:T(128)} %constant.128.clone.1, s32[]{:T(128)S(6)} %select_n.122, s32[]{:T(128)} %constant.128.clone.1) | dynamic-update-slice | bytes 65540 | tf_op jit(solution)/shard_map/dynamic_update_slice | solution.py:15
  146.4 1.8 copy.55
  148.2 7.5 %dynamic_update_slice.55 = bf16[64,128,32]{1,0,2:T(8,128)(2,1)S(1)} dynamic-update-slice(bf16[64,128,32]{1,0,2:T(8,128)(2,1)S(1)} %dynamic_update_slice.54, bf16[64,8,32]{1,0,2:T(8,128)(2,1)S(1)} %copy.55, s32[]{:T(128)} %constant.128.clone.1, s32[]{:T(128)S(6)} %select_n.124, s32[]{:T(128)} %constant.128.clone.1) | dynamic-update-slice | bytes 65540 | tf_op jit(solution)/shard_map/dynamic_update_slice | solution.py:15
  155.6 1.8 copy.56
  157.4 7.5 %dynamic_update_slice.56 = bf16[64,128,32]{1,0,2:T(8,128)(2,1)S(1)} dynamic-update-slice(bf16[64,128,32]{1,0,2:T(8,128)(2,1)S(1)} %dynamic_update_slice.55, bf16[64,8,32]{1,0,2:T(8,128)(2,1)S(1)} %copy.56, s32[]{:T(128)} %constant.128.clone.1, s32[]{:T(128)S(6)} %select_n.126, s32[]{:T(128)} %constant.128.clone.1) | dynamic-update-slice | bytes 65540 | tf_op jit(solution)/shard_map/dynamic_update_slice | solution.py:15
  164.9 1.8 copy.57
  166.7 7.5 %dynamic_update_slice.57 = bf16[64,128,32]{1,0,2:T(8,128)(2,1)S(1)} dynamic-update-slice(bf16[64,128,32]{1,0,2:T(8,128)(2,1)S(1)} %dynamic_update_slice.56, bf16[64,8,32]{1,0,2:T(8,128)(2,1)S(1)} %copy.57, s32[]{:T(128)} %constant.128.clone.1, s32[]{:T(128)S(6)} %select_n.128, s32[]{:T(128)} %constant.128.clone.1) | dynamic-update-slice | bytes 65540 | tf_op jit(solution)/shard_map/dynamic_update_slice | solution.py:15
  174.1 1.8 copy.58
  175.9 7.5 %dynamic_update_slice.58 = bf16[64,128,32]{1,0,2:T(8,128)(2,1)S(1)} dynamic-update-slice(bf16[64,128,32]{1,0,2:T(8,128)(2,1)S(1)} %dynamic_update_slice.57, bf16[64,8,32]{1,0,2:T(8,128)(2,1)S(1)} %copy.58, s32[]{:T(128)} %constant.128.clone.1, s32[]{:T(128)S(6)} %select_n.130, s32[]{:T(128)} %constant.128.clone.1) | dynamic-update-slice | bytes 65540 | tf_op jit(solution)/shard_map/dynamic_update_slice | solution.py:15
  183.4 1.8 copy.59
  185.2 7.5 %dynamic_update_slice.59 = bf16[64,128,32]{1,0,2:T(8,128)(2,1)S(1)} dynamic-update-slice(bf16[64,128,32]{1,0,2:T(8,128)(2,1)S(1)} %dynamic_update_slice.58, bf16[64,8,32]{1,0,2:T(8,128)(2,1)S(1)} %copy.59, s32[]{:T(128)} %constant.128.clone.1, s32[]{:T(128)S(6)} %select_n.132, s32[]{:T(128)} %constant.128.clone.1) | dynamic-update-slice | bytes 65540 | tf_op jit(solution)/shard_map/dynamic_update_slice | solution.py:15
  192.7 1.8 copy.60
  194.4 7.7 %dynamic_update_slice.60 = bf16[64,128,32]{1,0,2:T(8,128)(2,1)S(1)} dynamic-update-slice(bf16[64,128,32]{1,0,2:T(8,128)(2,1)S(1)} %dynamic_update_slice.59, bf16[64,8,32]{1,0,2:T(8,128)(2,1)S(1)} %copy.60, s32[]{:T(128)} %constant.128.clone.1, s32[]{:T(128)S(6)} %select_n.134, s32[]{:T(128)} %constant.128.clone.1) | dynamic-update-slice | bytes 65540 | tf_op jit(solution)/shard_map/dynamic_update_slice | solution.py:15
  202.1 1.8 copy.61
  203.9 7.5 %dynamic_update_slice.61 = bf16[64,128,32]{1,0,2:T(8,128)(2,1)S(1)} dynamic-update-slice(bf16[64,128,32]{1,0,2:T(8,128)(2,1)S(1)} %dynamic_update_slice.60, bf16[64,8,32]{1,0,2:T(8,128)(2,1)S(1)} %copy.61, s32[]{:T(128)} %constant.128.clone.1, s32[]{:T(128)S(6)} %select_n.136, s32[]{:T(128)} %constant.128.clone.1) | dynamic-update-slice | bytes 65540 | tf_op jit(solution)/shard_map/dynamic_update_slice | solution.py:15
  211.4 1.8 copy.62
  213.2 7.5 %dynamic_update_slice.62 = bf16[64,128,32]{1,0,2:T(8,128)(2,1)S(1)} dynamic-update-slice(bf16[64,128,32]{1,0,2:T(8,128)(2,1)S(1)} %dynamic_update_slice.61, bf16[64,8,32]{1,0,2:T(8,128)(2,1)S(1)} %copy.62, s32[]{:T(128)} %constant.128.clone.1, s32[]{:T(128)S(6)} %select_n.138, s32[]{:T(128)} %constant.128.clone.1) | dynamic-update-slice | bytes 65540 | tf_op jit(solution)/shard_map/dynamic_update_slice | solution.py:15
  220.6 1.8 copy.63
  222.4 7.5 %dynamic_update_slice.63 = bf16[64,128,32]{1,0,2:T(8,128)(2,1)S(1)} dynamic-update-slice(bf16[64,128,32]{1,0,2:T(8,128)(2,1)S(1)} %dynamic_update_slice.62, bf16[64,8,32]{1,0,2:T(8,128)(2,1)S(1)} %copy.63, s32[]{:T(128)} %constant.128.clone.1, s32[]{:T(128)S(6)} %select_n.140, s32[]{:T(128)} %constant.128.clone.1) | dynamic-update-slice | bytes 65540 | tf_op jit(solution)/shard_map/dynamic_update_slice | solution.py:15
  229.9 1.8 copy.64
  231.7 7.5 %dynamic_update_slice.64 = bf16[64,128,32]{1,0,2:T(8,128)(2,1)S(1)} dynamic-update-slice(bf16[64,128,32]{1,0,2:T(8,128)(2,1)S(1)} %dynamic_update_slice.63, bf16[64,8,32]{1,0,2:T(8,128)(2,1)S(1)} %copy.64, s32[]{:T(128)} %constant.128.clone.1, s32[]{:T(128)S(6)} %select_n.142, s32[]{:T(128)} %constant.128.clone.1) | dynamic-update-slice | bytes 65540 | tf_op jit(solution)/shard_map/dynamic_update_slice | solution.py:15
  239.2 1.8 copy.65
  240.9 7.5 %dynamic_update_slice.65 = bf16[64,128,32]{1,0,2:T(8,128)(2,1)S(1)} dynamic-update-slice(bf16[64,128,32]{1,0,2:T(8,128)(2,1)S(1)} %dynamic_update_slice.64, bf16[64,8,32]{1,0,2:T(8,128)(2,1)S(1)} %copy.65, s32[]{:T(128)} %constant.128.clone.1, s32[]{:T(128)S(6)} %select_n.144, s32[]{:T(128)} %constant.128.clone.1) | dynamic-update-slice | bytes 65540 | tf_op jit(solution)/shard_map/dynamic_update_slice | solution.py:15
  248.4 1.8 copy.66
  250.2 7.5 %dynamic_update_slice.66 = bf16[64,128,32]{1,0,2:T(8,128)(2,1)S(1)} dynamic-update-slice(bf16[64,128,32]{1,0,2:T(8,128)(2,1)S(1)} %dynamic_update_slice.65, bf16[64,8,32]{1,0,2:T(8,128)(2,1)S(1)} %copy.66, s32[]{:T(128)} %constant.128.clone.1, s32[]{:T(128)S(6)} %select_n.146, s32[]{:T(128)} %constant.128.clone.1) | dynamic-update-slice | bytes 65540 | tf_op jit(solution)/shard_map/dynamic_update_slice | solution.py:15
  257.7 1.8 copy.67
  259.5 7.7 %dynamic_update_slice.67 = bf16[64,128,32]{1,0,2:T(8,128)(2,1)S(1)} dynamic-update-slice(bf16[64,128,32]{1,0,2:T(8,128)(2,1)S(1)} %dynamic_update_slice.66, bf16[64,8,32]{1,0,2:T(8,128)(2,1)S(1)} %copy.67, s32[]{:T(128)} %constant.128.clone.1, s32[]{:T(128)S(6)} %select_n.148, s32[]{:T(128)} %constant.128.clone.1) | dynamic-update-slice | bytes 65540 | tf_op jit(solution)/shard_map/dynamic_update_slice | solution.py:15
  267.2 0.7 fusion.10
  268.1 0.7 convert_bitcast_fusion
  268.8 1.4 copy.69
  270.1 1.5 fusion.8
  271.7 1.2 copy.86
  273.7 1.0 fusion.21
  (63 shorter events, 3.9 us)
Async XLA Ops:
  7.2 8.6 %copy-start = (bf16[1024,128]{1,0:T(8,128)(2,1)S(1)}, bf16[1024,128]{1,0:T(8,128)(2,1)}, u32[]{:S(2)}) copy-start(bf16[1024,128]{1,0:T(8,128)(2,1)} %param.9) | copy-start | bytes 786436
  7.2 8.6 %copy-start.15 = (bf16[8,128,128]{2,1,0:T(8,128)(2,1)S(1)}, bf16[8,128,128]{2,1,0:T(8,128)(2,1)}, u32[]{:S(2)}) copy-start(bf16[8,128,128]{2,1,0:T(8,128)(2,1)} %param.11) | copy-start | bytes 786436
  7.2 264.5 %reduce-scatter.4.cloned.1.call-start = ((), (), s32[]{:S(2)}) async-start(), calls=%async_computation.1 | async-start | bytes 1114112
  13.0 0.6 copy-start.12
  19.3 8.5 %collective-permute-start = (bf16[64,8,32]{2,1,0:T(8,128)(2,1)}, bf16[64,8,32]{2,1,0:T(8,128)(2,1)}, u32[]{:S(2)}, u32[]{:S(2)}) collective-permute-start(bf16[64,8,32]{2,1,0:T(8,128)(2,1)} %get-tuple-element.27), channel_id=1, source_target_pairs={{0,1},{1,2},{2,3},{3,4},{4,5},{5,6},{6,7},{7,8},{8,9},{9,10},{10,1... | collective-permute-start | bytes 98312 | tf_op jit(solution)/shard_map/ppermute | solution.py:14
  27.8 7.4 %collective-permute-start.1 = (bf16[64,8,32]{2,1,0:T(8,128)(2,1)}, bf16[64,8,32]{2,1,0:T(8,128)(2,1)}, u32[]{:S(2)}, u32[]{:S(2)}) collective-permute-start(bf16[64,8,32]{2,1,0:T(8,128)(2,1)} %collective-permute-done), channel_id=1, source_target_pairs={{0,1},{1,2},{2,3},{3,4},{4,5},{5,6},{6,7},{7,8},{8,9},{9,10},{10,1... | collective-permute-start | bytes 98312 | tf_op jit(solution)/shard_map/ppermute | solution.py:14
  35.2 7.4 %collective-permute-start.2 = (bf16[64,8,32]{2,1,0:T(8,128)(2,1)}, bf16[64,8,32]{2,1,0:T(8,128)(2,1)}, u32[]{:S(2)}, u32[]{:S(2)}) collective-permute-start(bf16[64,8,32]{2,1,0:T(8,128)(2,1)} %collective-permute-done.1), channel_id=1, source_target_pairs={{0,1},{1,2},{2,3},{3,4},{4,5},{5,6},{6,7},{7,8},{8,9},{9,10},{10,1... | collective-permute-start | bytes 98312 | tf_op jit(solution)/shard_map/ppermute | solution.py:14
  42.6 7.3 %collective-permute-start.3 = (bf16[64,8,32]{2,1,0:T(8,128)(2,1)}, bf16[64,8,32]{2,1,0:T(8,128)(2,1)S(1)}, u32[]{:S(2)}, u32[]{:S(2)}) collective-permute-start(bf16[64,8,32]{2,1,0:T(8,128)(2,1)} %collective-permute-done.2), channel_id=1, source_target_pairs={{0,1},{1,2},{2,3},{3,4},{4,5},{5,6},{6,7},{7,8},{8,9},{9,10},{10,1... | collective-permute-start | bytes 98312 | tf_op jit(solution)/shard_map/ppermute | solution.py:14
  49.9 73.1 %copy-start.2 = (bf16[64,8,32]{2,1,0:T(8,128)(2,1)}, bf16[64,8,32]{2,1,0:T(8,128)(2,1)S(1)}, u32[]{:S(2)}) copy-start(bf16[64,8,32]{2,1,0:T(8,128)(2,1)S(1)} %collective-permute-done.3) | copy-start | bytes 98308
  49.9 7.3 %collective-permute-start.4 = (bf16[64,8,32]{2,1,0:T(8,128)(2,1)S(1)}, bf16[64,8,32]{2,1,0:T(8,128)(2,1)S(1)}, u32[]{:S(2)}, u32[]{:S(2)}) collective-permute-start(bf16[64,8,32]{2,1,0:T(8,128)(2,1)S(1)} %collective-permute-done.3), channel_id=1, source_target_pairs={{0,1},{1,2},{2,3},{3,4},{4,5},{5,6},{6,7},{7,8},{8,9},{9,10},{10,1... | collective-permute-start | bytes 98312 | tf_op jit(solution)/shard_map/ppermute | solution.py:14
  57.2 65.8 %copy-start.3 = (bf16[64,8,32]{2,1,0:T(8,128)(2,1)}, bf16[64,8,32]{2,1,0:T(8,128)(2,1)S(1)}, u32[]{:S(2)}) copy-start(bf16[64,8,32]{2,1,0:T(8,128)(2,1)S(1)} %collective-permute-done.4) | copy-start | bytes 98308
  57.2 7.2 %collective-permute-start.5 = (bf16[64,8,32]{2,1,0:T(8,128)(2,1)S(1)}, bf16[64,8,32]{2,1,0:T(8,128)(2,1)S(1)}, u32[]{:S(2)}, u32[]{:S(2)}) collective-permute-start(bf16[64,8,32]{2,1,0:T(8,128)(2,1)S(1)} %collective-permute-done.4), channel_id=1, source_target_pairs={{0,1},{1,2},{2,3},{3,4},{4,5},{5,6},{6,7},{7,8},{8,9},{9,10},{10,1... | collective-permute-start | bytes 98312 | tf_op jit(solution)/shard_map/ppermute | solution.py:14
  64.4 58.6 %copy-start.4 = (bf16[64,8,32]{2,1,0:T(8,128)(2,1)}, bf16[64,8,32]{2,1,0:T(8,128)(2,1)S(1)}, u32[]{:S(2)}) copy-start(bf16[64,8,32]{2,1,0:T(8,128)(2,1)S(1)} %collective-permute-done.5) | copy-start | bytes 98308
  64.4 7.2 %collective-permute-start.6 = (bf16[64,8,32]{2,1,0:T(8,128)(2,1)S(1)}, bf16[64,8,32]{2,1,0:T(8,128)(2,1)S(1)}, u32[]{:S(2)}, u32[]{:S(2)}) collective-permute-start(bf16[64,8,32]{2,1,0:T(8,128)(2,1)S(1)} %collective-permute-done.5), channel_id=1, source_target_pairs={{0,1},{1,2},{2,3},{3,4},{4,5},{5,6},{6,7},{7,8},{8,9},{9,10},{10,1... | collective-permute-start | bytes 98312 | tf_op jit(solution)/shard_map/ppermute | solution.py:14
  71.6 51.4 %copy-start.5 = (bf16[64,8,32]{2,1,0:T(8,128)(2,1)}, bf16[64,8,32]{2,1,0:T(8,128)(2,1)S(1)}, u32[]{:S(2)}) copy-start(bf16[64,8,32]{2,1,0:T(8,128)(2,1)S(1)} %collective-permute-done.6) | copy-start | bytes 98308
  71.6 7.4 %collective-permute-start.7 = (bf16[64,8,32]{2,1,0:T(8,128)(2,1)S(1)}, bf16[64,8,32]{2,1,0:T(8,128)(2,1)S(1)}, u32[]{:S(2)}, u32[]{:S(2)}) collective-permute-start(bf16[64,8,32]{2,1,0:T(8,128)(2,1)S(1)} %collective-permute-done.6), channel_id=1, source_target_pairs={{0,1},{1,2},{2,3},{3,4},{4,5},{5,6},{6,7},{7,8},{8,9},{9,10},{10,1... | collective-permute-start | bytes 98312 | tf_op jit(solution)/shard_map/ppermute | solution.py:14
  79.0 46.1 %copy-start.6 = (bf16[64,8,32]{2,1,0:T(8,128)(2,1)}, bf16[64,8,32]{2,1,0:T(8,128)(2,1)S(1)}, u32[]{:S(2)}) copy-start(bf16[64,8,32]{2,1,0:T(8,128)(2,1)S(1)} %collective-permute-done.7) | copy-start | bytes 98308
  79.0 7.1 %collective-permute-start.8 = (bf16[64,8,32]{2,1,0:T(8,128)(2,1)S(1)}, bf16[64,8,32]{2,1,0:T(8,128)(2,1)S(1)}, u32[]{:S(2)}, u32[]{:S(2)}) collective-permute-start(bf16[64,8,32]{2,1,0:T(8,128)(2,1)S(1)} %collective-permute-done.7), channel_id=1, source_target_pairs={{0,1},{1,2},{2,3},{3,4},{4,5},{5,6},{6,7},{7,8},{8,9},{9,10},{10,1... | collective-permute-start | bytes 98312 | tf_op jit(solution)/shard_map/ppermute | solution.py:14
  86.1 39.0 %copy-start.7 = (bf16[64,8,32]{2,1,0:T(8,128)(2,1)}, bf16[64,8,32]{2,1,0:T(8,128)(2,1)S(1)}, u32[]{:S(2)}) copy-start(bf16[64,8,32]{2,1,0:T(8,128)(2,1)S(1)} %collective-permute-done.8) | copy-start | bytes 98308
  86.1 7.1 %collective-permute-start.9 = (bf16[64,8,32]{2,1,0:T(8,128)(2,1)S(1)}, bf16[64,8,32]{2,1,0:T(8,128)(2,1)S(1)}, u32[]{:S(2)}, u32[]{:S(2)}) collective-permute-start(bf16[64,8,32]{2,1,0:T(8,128)(2,1)S(1)} %collective-permute-done.8), channel_id=1, source_target_pairs={{0,1},{1,2},{2,3},{3,4},{4,5},{5,6},{6,7},{7,8},{8,9},{9,10},{10,1... | collective-permute-start | bytes 98312 | tf_op jit(solution)/shard_map/ppermute | solution.py:14
  93.2 31.9 %copy-start.8 = (bf16[64,8,32]{2,1,0:T(8,128)(2,1)}, bf16[64,8,32]{2,1,0:T(8,128)(2,1)S(1)}, u32[]{:S(2)}) copy-start(bf16[64,8,32]{2,1,0:T(8,128)(2,1)S(1)} %collective-permute-done.9) | copy-start | bytes 98308
  93.2 7.1 %collective-permute-start.10 = (bf16[64,8,32]{2,1,0:T(8,128)(2,1)S(1)}, bf16[64,8,32]{2,1,0:T(8,128)(2,1)S(1)}, u32[]{:S(2)}, u32[]{:S(2)}) collective-permute-start(bf16[64,8,32]{2,1,0:T(8,128)(2,1)S(1)} %collective-permute-done.9), channel_id=1, source_target_pairs={{0,1},{1,2},{2,3},{3,4},{4,5},{5,6},{6,7},{7,8},{8,9},{9,10},{10,1... | collective-permute-start | bytes 98312 | tf_op jit(solution)/shard_map/ppermute | solution.py:14
  100.3 24.8 %copy-start.9 = (bf16[64,8,32]{2,1,0:T(8,128)(2,1)}, bf16[64,8,32]{2,1,0:T(8,128)(2,1)S(1)}, u32[]{:S(2)}) copy-start(bf16[64,8,32]{2,1,0:T(8,128)(2,1)S(1)} %collective-permute-done.10) | copy-start | bytes 98308
  100.3 7.1 %collective-permute-start.11 = (bf16[64,8,32]{2,1,0:T(8,128)(2,1)S(1)}, bf16[64,8,32]{2,1,0:T(8,128)(2,1)S(1)}, u32[]{:S(2)}, u32[]{:S(2)}) collective-permute-start(bf16[64,8,32]{2,1,0:T(8,128)(2,1)S(1)} %collective-permute-done.10), channel_id=1, source_target_pairs={{0,1},{1,2},{2,3},{3,4},{4,5},{5,6},{6,7},{7,8},{8,9},{9,10},{10,1... | collective-permute-start | bytes 98312 | tf_op jit(solution)/shard_map/ppermute | solution.py:14
  107.4 0.6 copy-start.10
  108.1 7.1 %collective-permute-start.12 = (bf16[64,8,32]{2,1,0:T(8,128)(2,1)S(1)}, bf16[64,8,32]{2,1,0:T(8,128)(2,1)S(1)}, u32[]{:S(2)}, u32[]{:S(2)}) collective-permute-start(bf16[64,8,32]{2,1,0:T(8,128)(2,1)S(1)} %collective-permute-done.11), channel_id=1, source_target_pairs={{0,1},{1,2},{2,3},{3,4},{4,5},{5,6},{6,7},{7,8},{8,9},{9,10},{10,1... | collective-permute-start | bytes 98312 | tf_op jit(solution)/shard_map/ppermute | solution.py:14
  115.1 0.6 copy-start.11
  115.8 7.2 %collective-permute-start.13 = (bf16[64,8,32]{2,1,0:T(8,128)(2,1)S(1)}, bf16[64,8,32]{2,1,0:T(8,128)(2,1)}, u32[]{:S(2)}, u32[]{:S(2)}) collective-permute-start(bf16[64,8,32]{2,1,0:T(8,128)(2,1)S(1)} %collective-permute-done.12), channel_id=1, source_target_pairs={{0,1},{1,2},{2,3},{3,4},{4,5},{5,6},{6,7},{7,8},{8,9},{9,10},{10,1... | collective-permute-start | bytes 98312 | tf_op jit(solution)/shard_map/ppermute | solution.py:14
  123.0 134.7 %collective-permute-start.14 = (bf16[64,8,32]{2,1,0:T(8,128)(2,1)}, bf16[64,8,32]{2,1,0:T(8,128)(2,1)}, u32[]{:S(2)}, u32[]{:S(2)}) collective-permute-start(bf16[64,8,32]{2,1,0:T(8,128)(2,1)} %collective-permute-done.13), channel_id=1, source_target_pairs={{0,1},{1,2},{2,3},{3,4},{4,5},{5,6},{6,7},{7,8},{8,9},{9,10},{10,1... | collective-permute-start | bytes 98312 | tf_op jit(solution)/shard_map/ppermute | solution.py:14
  268.8 1.4 copy-start.16
  271.6 1.6 copy-start.1
  271.6 1.6 copy-start.13
  271.6 1.6 copy-start.14
Sparse Core Ops, SparseCore 0:
  19.4 61.7 reduce-scatter.3
